TPU v7x, 512 devices: a whole 4x4x16 slice. The times are simulated.
512 devices in a mesh: rep: 4 (over y), own: 128 (over x, z, core).
Axes of the slice: x: 4, y: 4, z: 16, core: 2. Of those that a mesh axis runs over, the one named last changes fastest.
Arguments:
- owners: int32 [256, 1], replicated, may hold values from 0 to 127; in each aligned block of 256 rows (0 to 255, 256 to 511, ...) at most 4 rows name the same one
- inner_dense: float32 [4, 256, 65536], P('rep', None, 'own'), may hold values from -6 to 6
- anchor_dense: float32 [256, 65536], P(None, 'own'), may hold values from -6 to 6
- momentum_dense: float32 [512, 65536], P('own'), may hold values from -6 to 6
- inner_emb: float32 [4, 25600, 1024], P('rep', 'own'), may hold values from -6 to 6
- anchor_emb: float32 [25600, 1024], P('own'), may hold values from -6 to 6
- momentum_emb: float32 [25600, 64], P('own'), may hold values from -6 to 6
- basis: float32 [1024, 64], replicated, may hold values from -0.1875 to 0.1875
Outputs:
- new_dense: float32 [256, 65536], P(None, 'own')
- new_momentum_dense: float32 [512, 65536], P('own')
- new_emb: float32 [25600, 1024], P('own')
- new_momentum_emb: float32 [25600, 64], P('own')
Inputs may be any that keep to these rules, and one draw needn't show every extreme that they name: `owners`: each owner position owns at most 4 blocks, and some position owns exactly 4.
All inputs are finite; a program needn't handle non-finite values.
Results may differ from a plain program's by a relative error of at most 0.00011.
Values sent between devices are 32-bit elements; how exact they have to be, the bound alone decides.
A program may use at most 64 MiB of HBM per device.

v0:
```python
import jax
import jax.numpy as jnp
from jax import lax
from jax.sharding import PartitionSpec as P

outer_rate = 0.7
momentum_decay = 0.9


def slot_positions(owner_column, owner_count):
    owner_flat = owner_column[:, 0]
    onehot = (owner_flat[:, None] == jnp.arange(owner_count, dtype=jnp.int32)[None, :]).astype(
        jnp.int32
    )
    running = jnp.cumsum(onehot, axis=0) - onehot
    slot_of = jnp.sum(running * onehot, axis=1)
    return (owner_flat, slot_of)


def per_device(
    owners, inner_dense, anchor_dense, momentum_dense, inner_emb, anchor_emb, momentum_emb, basis
):
    owner_count = lax.axis_size("own")
    groups = lax.axis_size("rep")
    my_index = lax.axis_index("own")
    slot_count = momentum_dense.shape[0]
    flat_len = momentum_dense.shape[1]
    piece_len = anchor_dense.shape[1]
    owner_flat, slot_of = slot_positions(owners, owner_count)
    position = slot_of * owner_count + owner_flat
    owned_count = jnp.sum((owner_flat == my_index).astype(jnp.int32))
    live_mask = (jnp.arange(slot_count, dtype=jnp.int32) < owned_count)[:, None]
    difference = anchor_dense - inner_dense[0]
    factor = jnp.dot(
        anchor_emb - inner_emb[0],
        basis,
        precision=lax.Precision.HIGHEST,
        preferred_element_type=jnp.float32,
    )
    summed, factor_sum = lax.psum((difference, factor), "rep")
    mean_grad = summed / groups
    filled = (
        jnp.zeros((slot_count * owner_count, piece_len), jnp.float32).at[position].set(mean_grad)
    )
    received = lax.all_to_all(
        filled.reshape(slot_count, owner_count, piece_len),
        "own",
        split_axis=1,
        concat_axis=1,
        tiled=True,
    ).reshape(slot_count, flat_len)
    new_momentum_dense = jnp.where(live_mask, momentum_decay * momentum_dense + received, 0.0)
    slot_update = received + momentum_decay * new_momentum_dense
    returned = lax.all_to_all(
        slot_update.reshape(slot_count, owner_count, piece_len),
        "own",
        split_axis=1,
        concat_axis=1,
        tiled=True,
    )
    update = returned.reshape(slot_count * owner_count, piece_len)[position]
    new_dense = anchor_dense - outer_rate * update
    mean_factor = factor_sum / groups
    new_momentum_emb = momentum_decay * momentum_emb + mean_factor
    emb_update = mean_factor + momentum_decay * new_momentum_emb
    new_emb = anchor_emb - outer_rate * jnp.dot(
        emb_update, basis.T, precision=lax.Precision.HIGHEST, preferred_element_type=jnp.float32
    )
    return (new_dense, new_momentum_dense, new_emb, new_momentum_emb)


def solution(mesh):
    placed = (
        P(),
        P("rep", None, "own"),
        P(None, "own"),
        P("own", None),
        P("rep", "own", None),
        P("own", None),
        P("own", None),
        P(),
    )
    return jax.shard_map(
        per_device,
        mesh=mesh,
        in_specs=placed,
        out_specs=(P(None, "own"), P("own", None), P("own", None), P("own", None)),
        check_vma=False,
    )
```

profile of v0, /device:TPU:1, one launch (start us, length us, event | category | flops | bytes accessed | tf_op | source)
XLA Modules:
  0.0 223.9 jit_solution(11279165621121968072)
XLA Ops:
  7.2 0.0 copy-start
  7.2 0.0 all-reduce.2.cloned.1.call-start
  7.2 2.1 bitcast_subtract_fusion.2
  9.3 0.0 all-reduce.2.cloned.1.call-update
  9.4 0.0 copy-start.7
  9.4 0.7 copy-done.7
  10.0 0.1 copy.15
  10.2 0.2 fusion.6
  10.5 0.2 fusion.8
  10.7 62.0 %all-reduce.2.cloned.1.call-done = f32[256,512]{1,0:T(8,128)} async-done(((f32[256,512]{1,0:T(8,128)}), f32[256,512]{1,0:T(8,128)}) %all-reduce.2.cloned.1.call-update) | async-done | bytes 524304 | tf_op jit(solution)/shard_map/psum | solution.py:40
  72.6 2.2 scatter_custom_fusion
  74.9 1.6 copy.17
  76.5 18.9 %all-to-all-start = ((f32[4,128,512]{2,0,1:T(4,128)}), f32[4,128,512]{2,0,1:T(4,128)S(1)}, u32[]{:S(2)}, u32[]{:S(2)}) async-start(f32[4,128,512]{2,0,1:T(4,128)} %copy.17), calls=%async_computation | async-start | bytes 2097152 | tf_op jit(solution)/shard_map/all_to_all | solution.py:45
  95.5 0.6 fusion.16
  96.1 0.6 iota_compare_fusion.1
  96.8 53.1 %all-to-all-done = f32[4,128,512]{2,0,1:T(4,128)S(1)} async-done(((f32[4,128,512]{2,0,1:T(4,128)}), f32[4,128,512]{2,0,1:T(4,128)S(1)}, u32[]{:S(2)}, u32[]{:S(2)}) %all-to-all-start) | async-done | bytes 1048608 | tf_op jit(solution)/shard_map/all_to_all | solution.py:45
  149.9 0.0 copy-done.3
  149.9 2.0 multiply_add_fusion
  151.9 8.5 %all-to-all-start.1 = ((f32[4,128,512]{2,0,1:T(4,128)}), f32[4,128,512]{2,0,1:T(4,128)S(1)}, u32[]{:S(2)}, u32[]{:S(2)}) async-start(f32[4,128,512]{2,0,1:T(4,128)} %bitcast.10), calls=%async_computation.1 | async-start | bytes 2097152 | tf_op jit(solution)/shard_map/all_to_all | solution.py:54
  160.4 0.0 copy-done
  160.4 0.0 copy-done.1
  160.4 0.0 copy-done.4
  160.4 0.9 fusion.1
  161.3 14.0 %psum.15 = f32[200,64]{0,1:T(8,128)S(1)} all-reduce(f32[200,64]{0,1:T(8,128)S(1)} %fusion.1), channel_id=1, replica_groups=mesh['rep'=4,'own'=128] {'rep'}, use_global_device_ids=true, to_apply=%region_6.7 | all-reduce | flops 12800 | bytes 102400 | tf_op jit(solution)/shard_map/psum | solution.py:40
  175.4 0.0 copy-start.5
  175.4 1.8 fusion
  177.2 37.6 %all-to-all-done.1 = f32[4,128,512]{2,0,1:T(4,128)S(1)} async-done(((f32[4,128,512]{2,0,1:T(4,128)}), f32[4,128,512]{2,0,1:T(4,128)S(1)}, u32[]{:S(2)}, u32[]{:S(2)}) %all-to-all-start.1) | async-done | bytes 1048608 | tf_op jit(solution)/shard_map/all_to_all | solution.py:54
  214.8 0.3 copy.18
  215.1 0.0 copy-start.2
  215.2 1.0 gather_fusion
  216.1 0.1 copy-done.2
  216.2 0.9 multiply_subtract_fusion
  (16 shorter events, 0.1 us)
Async XLA Ops:
  7.2 153.2 %copy-start = (f32[1024,64]{0,1:T(8,128)S(1)}, f32[1024,64]{0,1:T(8,128)}, u32[]{:S(2)}) copy-start(f32[1024,64]{0,1:T(8,128)} %param.15) | copy-start | bytes 786436
  7.2 65.5 %all-reduce.2.cloned.1.call-start = ((), (), s32[]{:S(2)}) async-start(), calls=%async_computation.2 | async-start | bytes 1048576 | tf_op jit(solution)/shard_map/psum | solution.py:40
  9.4 0.7 copy-start.7
  76.5 73.4 %copy-start.3 = (f32[4,65536]{1,0:T(4,128)S(1)}, f32[4,65536]{1,0:T(4,128)}, u32[]{:S(2)}) copy-start(f32[4,65536]{1,0:T(4,128)} %param.11) | copy-start | bytes 3145732
  76.5 73.4 %all-to-all-start = ((f32[4,128,512]{2,0,1:T(4,128)}), f32[4,128,512]{2,0,1:T(4,128)S(1)}, u32[]{:S(2)}, u32[]{:S(2)}) async-start(f32[4,128,512]{2,0,1:T(4,128)} %copy.17), calls=%async_computation | async-start | bytes 2097152 | tf_op jit(solution)/shard_map/all_to_all | solution.py:45
  151.8 8.6 %copy-start.1 = (f32[200,1024]{1,0:T(8,128)S(1)}, f32[200,1024]{1,0:T(8,128)}, u32[]{:S(2)}) copy-start(f32[200,1024]{1,0:T(8,128)} %param.13) | copy-start | bytes 2457604
  151.9 8.6 %copy-start.4 = (f32[1,200,1024]{2,1,0:T(8,128)S(1)}, f32[1,200,1024]{2,1,0:T(8,128)}, u32[]{:S(2)}) copy-start(f32[1,200,1024]{2,1,0:T(8,128)} %param.12) | copy-start | bytes 2457604
  151.9 62.9 %all-to-all-start.1 = ((f32[4,128,512]{2,0,1:T(4,128)}), f32[4,128,512]{2,0,1:T(4,128)S(1)}, u32[]{:S(2)}, u32[]{:S(2)}) async-start(f32[4,128,512]{2,0,1:T(4,128)} %bitcast.10), calls=%async_computation.1 | async-start | bytes 2097152 | tf_op jit(solution)/shard_map/all_to_all | solution.py:54
  161.3 14.0 %copy-start.6 = (f32[200,64]{0,1:T(8,128)S(1)}, f32[200,64]{0,1:T(8,128)}, u32[]{:S(2)}) copy-start(f32[200,64]{0,1:T(8,128)} %param.14) | copy-start | bytes 153604
  175.4 1.8 copy-start.5
  215.1 1.0 copy-start.2
Sparse Core Ops, SparseCore 0:
  10.9 61.6 all-reduce.1
where the time goes:
time: 225 us; the launch traced here: 224 us
  waiting for transfers between devices  153 us (68%)
  starting transfers between devices  27.5 us (12%)
  between operations  14.2 us (6%)
  blocking collectives  14 us (6%)
  other arithmetic  8.92 us (4%)
  local copies, waits for them, and re-layouts  3.86 us (2%)
  matrix products  2.67 us (1%)
    psum x1, waiting for transfers between devices, per_device(): summed, factor_sum = lax.psum((difference, factor), 'rep')  62 us
    all_to_all x1, waiting for transfers between devices, per_device(): lax.all_to_all(filled.reshape(slot_count, owner_count, piece_len), 'own',...  53.1 us
    all_to_all x1, waiting for transfers between devices, per_device(): lax.all_to_all(slot_update.reshape(slot_count, owner_count, piece_len), '...  37.6 us
    all_to_all x1, starting transfers between devices, per_device(): lax.all_to_all(filled.reshape(slot_count, owner_count, piece_len), 'own',...  18.9 us
    psum x1, blocking collectives, per_device(): summed, factor_sum = lax.psum((difference, factor), 'rep')  14 us
    all_to_all x1, starting transfers between devices, per_device(): lax.all_to_all(slot_update.reshape(slot_count, owner_count, piece_len), '...  8.53 us
  transfers between devices with their start and end apart: 3, of which 3 were waited for; matrix products, arithmetic and copies ran while one was open for 2% of the time, Pallas kernels for 0%

commit v1 on v0

v1 whole, which is shorter than its diff:
```python
import jax
import jax.numpy as jnp
from jax import lax
from jax.experimental import pallas as pl
from jax.experimental.pallas import tpu as pltpu
from jax.sharding import PartitionSpec as P

MESH = pl.DeviceIdType.MESH
RATE = 0.7
DECAY = 0.9
NX, NZ, NC, NR, NS = 4, 16, 2, 4, 4
LANES = 128
F32 = jnp.float32
BF16 = jnp.bfloat16
SEND_ORDER = (8, 7, 9, 6, 10, 5, 11, 4, 12, 3, 13, 2, 14, 1, 15)
RANGES = ((6, 11), (3, 6), (11, 14), (14, 16), (0, 3))
GROUPS_Z = ((0,), (1, 2), (3, 4))


def split3(v):
    high = v.astype(BF16)
    rest = v - high.astype(F32)
    mid = rest.astype(BF16)
    low = (rest - mid.astype(F32)).astype(BF16)
    return high, mid, low


def select_rows(onehot, v):
    high, mid, low = split3(v)
    total = jnp.dot(onehot, low, preferred_element_type=F32)
    total = total + jnp.dot(onehot, mid, preferred_element_type=F32)
    return total + jnp.dot(onehot, high, preferred_element_type=F32)


def kernel(
    owners_hbm, inner_hbm, anchor_hbm, mom_hbm, iemb_hbm, aemb_hbm, memb_hbm, basis_hbm,
    nd_out, nm_out, ne_out, nme_out,
    owners, inq, anq, mom_v, ie, ae, memb, basis,
    rly, yin, gq, pack1, pick1, m1, m2, g0, g1, g2, fac,
    loc, rs_recv, mz_recv, mp_recv, gz_recv, gp_recv, gy_recv, gf_recv, nd_recv, f_recv, snd,
):
    own = lax.axis_index("own")
    rep = lax.axis_index("rep")
    c = lax.rem(own, NC)
    z = lax.rem(lax.div(own, NC), NZ)
    x = lax.div(own, NC * NZ)

    def position(px, pz, pc):
        return (px * NZ + pz) * NC + pc

    up = lax.rem(rep + 1, NR)
    down = lax.rem(rep + NR - 1, NR)
    across = lax.rem(rep + 2, NR)
    z_at = [lax.rem(z + d, NZ) for d in range(NZ)]
    z_peers = {d: {"rep": rep, "own": position(x, z_at[d], c)} for d in SEND_ORDER}
    plane = []
    for dx in range(NX):
        for dc in range(NC):
            if dx or dc:
                px, pc = lax.rem(x + dx, NX), lax.rem(c + dc, NC)
                plane.append((px, pc, {"rep": rep, "own": position(px, z, pc)}))
    to_up = {"rep": up, "own": own}
    to_down = {"rep": down, "own": own}
    to_across = {"rep": across, "own": own}

    def local(src, dst, sem):
        copy = pltpu.make_async_copy(src, dst, sem)
        copy.start()

    def arrived(ref, sem):
        pltpu.make_async_copy(ref, ref, sem).wait()

    def send(src, dst, send_sem, recv_sem, peer):
        pltpu.make_async_remote_copy(
            src_ref=src, dst_ref=dst, send_sem=send_sem, recv_sem=recv_sem,
            device_id=peer, device_id_type=MESH,
        ).start()

    def columns(r):
        return pl.ds(pl.multiple_of(r * LANES, LANES), LANES)

    half = (pl.ds(0, 128), pl.ds(128, 128))

    barrier = pltpu.get_barrier_semaphore()
    everyone = [z_peers[d] for d in SEND_ORDER] + [p[2] for p in plane]
    everyone += [to_up, to_down, to_across]
    for peer in everyone:
        pl.semaphore_signal(barrier, inc=1, device_id=peer, device_id_type=MESH)

    local(owners_hbm, owners, loc.at[0])
    local(inner_hbm.at[:, columns(rep)], inq, loc.at[1])
    local(anchor_hbm.at[:, columns(rep)], anq, loc.at[2])
    local(mom_hbm.at[:, z, :, rep], m1.at[0], mz_recv.at[4])
    local(iemb_hbm, ie, loc.at[4])
    local(aemb_hbm, ae, loc.at[5])
    local(basis_hbm, basis, loc.at[6])
    local(memb_hbm, memb, loc.at[7])
    local(mom_hbm, mom_v, loc.at[3])

    pl.semaphore_wait(barrier, len(everyone))

    send(inner_hbm.at[half[0], columns(across)], rly.at[0], snd.at[0], rs_recv.at[0], to_up)
    send(inner_hbm.at[half[1], columns(across)], rly.at[1], snd.at[0], rs_recv.at[1], to_down)
    send(inner_hbm.at[:, columns(up)], yin.at[0], snd.at[1], rs_recv.at[2], to_up)
    send(inner_hbm.at[:, columns(down)], yin.at[1], snd.at[1], rs_recv.at[3], to_down)

    def range_of(d):
        return next(i for i, (a, b) in enumerate(RANGES) if a <= d < b)

    for d in SEND_ORDER:
        send(mom_hbm.at[:, z_at[d], :, rep], m1.at[d], snd.at[2], mz_recv.at[range_of(d)], z_peers[d])

    arrived(owners, loc.at[0])
    names = owners[...]
    by_column = jnp.broadcast_to(names, (256, 256))
    by_row = by_column.T
    first = lax.broadcasted_iota(jnp.int32, (256, 256), 0)
    second = lax.broadcasted_iota(jnp.int32, (256, 256), 1)
    same = by_row == by_column
    slot_row = jnp.sum(jnp.where(same & (first < second), 1, 0), axis=0, keepdims=True)
    slot_column = jnp.sum(jnp.where(same & (second < first), 1, 0), axis=1, keepdims=True)

    def parts(p):
        return p >> 5, (p >> 1) & 15, p & 1

    ox, oz, oc = parts(names)
    pack_row = ((((oz - z) & 15) * NX + ox) * NC + oc) * NS + slot_row
    pack1[...] = jnp.where(
        lax.broadcasted_iota(jnp.int32, (512, 256), 0) == pack_row, 1.0, 0.0
    ).astype(BF16)
    ox, oz, oc = parts(by_row[:, 0:1])
    pick_column = ((ox * NZ + ((z - oz) & 15)) * NC + oc) * NS + slot_column
    pick1[...] = jnp.where(
        lax.broadcasted_iota(jnp.int32, (256, 512), 1) == pick_column, 1.0, 0.0
    ).astype(BF16)
    owned = jnp.sum(jnp.where(names == own, 1, 0), axis=1, keepdims=True)

    arrived(rly.at[0], rs_recv.at[0])
    send(rly.at[0], yin.at[2, half[0]], snd.at[3], rs_recv.at[4], to_up)
    arrived(rly.at[1], rs_recv.at[1])
    send(rly.at[1], yin.at[2, half[1]], snd.at[3], rs_recv.at[5], to_down)

    arrived(ie, loc.at[4])
    arrived(ae, loc.at[5])
    arrived(basis, loc.at[6])
    fac[rep] = lax.dot_general(
        basis[...], ae[...] - ie[...], (((1,), (1,)), ((), ())),
        precision=lax.Precision.HIGHEST, preferred_element_type=F32,
    )

    arrived(inq, loc.at[1])
    arrived(anq, loc.at[2])
    arrived(yin.at[0], rs_recv.at[2])
    arrived(yin.at[1], rs_recv.at[3])
    arrived(yin.at[2, half[0]], rs_recv.at[4])
    arrived(yin.at[2, half[1]], rs_recv.at[5])
    anchor = anq[...]
    grad = (anchor - inq[...]) + (anchor - yin[0])
    grad = (grad + (anchor - yin[1]) + (anchor - yin[2])) * 0.25
    gq[...] = grad
    g0[...] = select_rows(pack1[...], grad).reshape(NZ, NX, NC, NS, LANES)
    for d in SEND_ORDER:
        send(g0.at[d], g1.at[d], snd.at[4], gz_recv.at[range_of(d)], z_peers[d])
    local(g0.at[0], g1.at[0], gz_recv.at[4])
    for i, peer in enumerate((to_up, to_down, to_across)):
        send(fac.at[rep], fac.at[rep], snd.at[5], f_recv.at[i], peer)

    def spread(src, dst, i, send_sem, recv_sem):
        run = pl.ds(RANGES[i][0], RANGES[i][1] - RANGES[i][0])
        for px, pc, peer in plane:
            send(src.at[run, px, pc], dst.at[x, run, c], send_sem, recv_sem, peer)
        local(src.at[run, x, c], dst.at[x, run, c], recv_sem)

    def run_of(i):
        return pl.ds(RANGES[i][0], RANGES[i][1] - RANGES[i][0])

    def m_group(group):
        for i in GROUPS_Z[group]:
            arrived(m1.at[run_of(i)], mz_recv.at[i])
            spread(m1, m2, i, snd.at[6], mp_recv.at[i])

    def g_group(group):
        for i in GROUPS_Z[group]:
            arrived(g1.at[run_of(i)], gz_recv.at[i])
            spread(g1, g2.at[rep], i, snd.at[7], gp_recv.at[i])

    for group in range(3):
        m_group(group)
    for i in range(len(RANGES)):
        arrived(m2.at[:, run_of(i)], mp_recv.at[i])
    momentum = select_rows(pick1[...], m2[...].reshape(512, LANES))
    grad = gq[...]
    nd_out[:, columns(rep)] = anq[...] - RATE * (grad + DECAY * (DECAY * momentum + grad))

    def nd_part(r, h):
        return nd_out.at[half[h], columns(r)]

    send(nd_part(rep, 0), nd_part(rep, 0), snd.at[8], nd_recv.at[0], to_up)
    send(nd_part(rep, 1), nd_part(rep, 1), snd.at[8], nd_recv.at[3], to_down)
    send(nd_part(rep, 1), nd_part(rep, 1), snd.at[8], nd_recv.at[1], to_up)
    send(nd_part(rep, 0), nd_part(rep, 0), snd.at[8], nd_recv.at[2], to_down)

    arrived(memb, loc.at[7])
    arrived(fac.at[down], f_recv.at[0])
    arrived(fac.at[up], f_recv.at[1])
    arrived(fac.at[across], f_recv.at[2])
    mean_factor = ((fac[0] + fac[1]) + (fac[2] + fac[3])) * 0.25
    new_memb = DECAY * memb[...] + mean_factor
    nme_out[...] = new_memb
    emb_update = mean_factor + DECAY * new_memb
    ne_out[...] = ae[...] - RATE * lax.dot_general(
        emb_update, basis[...], (((0,), (0,)), ((), ())),
        precision=lax.Precision.HIGHEST, preferred_element_type=F32,
    )

    g_group(0)
    arrived(nd_part(down, 0), nd_recv.at[0])
    send(nd_part(down, 0), nd_part(down, 0), snd.at[9], nd_recv.at[4], to_up)
    arrived(nd_part(up, 1), nd_recv.at[3])
    send(nd_part(up, 1), nd_part(up, 1), snd.at[9], nd_recv.at[5], to_down)

    def g_part(r, i, h):
        return g2.at[r, pl.ds(2 * h, 2), run_of(i)]

    def g_share(group):
        for i in GROUPS_Z[group]:
            arrived(g2.at[rep, :, run_of(i)], gp_recv.at[i])
            send(g_part(rep, i, 0), g_part(rep, i, 0), snd.at[10], gy_recv.at[i, 0], to_up)
            send(g_part(rep, i, 1), g_part(rep, i, 1), snd.at[10], gy_recv.at[i, 3], to_down)
            send(g_part(rep, i, 1), g_part(rep, i, 1), snd.at[10], gy_recv.at[i, 1], to_up)
            send(g_part(rep, i, 0), g_part(rep, i, 0), snd.at[10], gy_recv.at[i, 2], to_down)

    def g_relay(group):
        for i in GROUPS_Z[group]:
            arrived(g_part(down, i, 0), gy_recv.at[i, 0])
            send(g_part(down, i, 0), g_part(down, i, 0), snd.at[11], gf_recv.at[i, 0], to_up)
            arrived(g_part(up, i, 1), gy_recv.at[i, 3])
            send(g_part(up, i, 1), g_part(up, i, 1), snd.at[11], gf_recv.at[i, 1], to_down)

    g_group(1)
    g_share(0)
    g_group(2)
    g_share(1)
    g_relay(0)
    g_share(2)
    g_relay(1)
    g_relay(2)

    arrived(nd_part(down, 1), nd_recv.at[1])
    arrived(nd_part(up, 0), nd_recv.at[2])
    arrived(nd_part(across, 0), nd_recv.at[4])
    arrived(nd_part(across, 1), nd_recv.at[5])
    arrived(mom_v, loc.at[3])
    for i in range(len(RANGES)):
        arrived(g_part(down, i, 1), gy_recv.at[i, 1])
        arrived(g_part(up, i, 0), gy_recv.at[i, 2])
        arrived(g_part(across, i, 0), gf_recv.at[i, 0])
        arrived(g_part(across, i, 1), gf_recv.at[i, 1])

    live = lax.broadcasted_iota(jnp.int32, (NS, LANES), 0) < owned

    def finish(d, carry):
        at = lax.rem(z + NZ - d, NZ)
        for px in range(NX):
            for pc in range(NC):
                for r in range(NR):
                    value = DECAY * mom_v[px, at, pc, r] + g2[r, px, d, pc]
                    nm_out[px, at, pc, r] = jnp.where(live, value, 0.0)
        return carry

    lax.fori_loop(0, NZ, finish, 0)

    arrived(rly, snd.at[0])
    arrived(yin.at[pl.ds(0, 2)], snd.at[1])
    arrived(m1.at[pl.ds(1, 15)], snd.at[2])
    arrived(rly, snd.at[3])
    arrived(g1.at[pl.ds(1, 15)], snd.at[4])
    arrived(fac.at[pl.ds(0, 3)], snd.at[5])
    arrived(m2.at[:, :, 0], snd.at[6])
    arrived(m2.at[pl.ds(0, 3), :, 0], snd.at[6])
    arrived(m2.at[:, :, 0], snd.at[7])
    arrived(m2.at[pl.ds(0, 3), :, 0], snd.at[7])
    arrived(yin.at[pl.ds(0, 2)], snd.at[8])
    arrived(rly, snd.at[9])
    arrived(g2.at[pl.ds(0, 2)], snd.at[10])
    arrived(g2.at[0], snd.at[11])


def per_device(
    owners, inner_dense, anchor_dense, momentum_dense, inner_emb, anchor_emb, momentum_emb, basis
):
    mom = momentum_dense.reshape(NS, 512, LANES).transpose(1, 0, 2)
    mom = mom.reshape(NX, NZ, NC, NR, NS, LANES)
    dma = pltpu.SemaphoreType.DMA
    vmem = pltpu.VMEM
    vocab, width = anchor_emb.shape
    rank = basis.shape[1]
    ranges = len(RANGES)
    new_dense, new_mom, new_emb, new_memb = pl.pallas_call(
        kernel,
        out_shape=(
            jax.ShapeDtypeStruct(anchor_dense.shape, F32),
            jax.ShapeDtypeStruct(mom.shape, F32),
            jax.ShapeDtypeStruct(anchor_emb.shape, F32),
            jax.ShapeDtypeStruct((rank, vocab), F32),
        ),
        in_specs=[pl.BlockSpec(memory_space=pltpu.HBM)] * 8,
        out_specs=[pl.BlockSpec(memory_space=pltpu.VMEM)] * 4,
        scratch_shapes=[
            vmem((1, 256), jnp.int32),
            vmem((256, LANES), F32),
            vmem((256, LANES), F32),
            vmem(mom.shape, F32),
            vmem((vocab, width), F32),
            vmem((vocab, width), F32),
            vmem((rank, vocab), F32),
            vmem((rank, width), F32),
            vmem((2, 128, LANES), F32),
            vmem((3, 256, LANES), F32),
            vmem((256, LANES), F32),
            vmem((512, 256), BF16),
            vmem((256, 512), BF16),
            vmem((NZ, NX, NC, NS, LANES), F32),
            vmem((NX, NZ, NC, NS, LANES), F32),
            vmem((NZ, NX, NC, NS, LANES), F32),
            vmem((NZ, NX, NC, NS, LANES), F32),
            vmem((NR, NX, NZ, NC, NS, LANES), F32),
            vmem((NR, rank, vocab), F32),
            dma((8,)),
            dma((6,)),
            dma((ranges,)),
            dma((ranges,)),
            dma((ranges,)),
            dma((ranges,)),
            dma((ranges, 4)),
            dma((ranges, 2)),
            dma((6,)),
            dma((3,)),
            dma((12,)),
        ],
        compiler_params=pltpu.CompilerParams(
            collective_id=0, has_side_effects=True, vmem_limit_bytes=32 * 1024 * 1024
        ),
    )(
        owners.reshape(1, 256), inner_dense[0], anchor_dense, mom, inner_emb[0], anchor_emb,
        momentum_emb.T, basis.T,
    )
    new_mom = new_mom.reshape(512, NS, LANES).transpose(1, 0, 2).reshape(momentum_dense.shape)
    return new_dense, new_mom, new_emb, new_memb.T


def solution(mesh):
    placed = (
        P(),
        P("rep", None, "own"),
        P(None, "own"),
        P("own", None),
        P("rep", "own", None),
        P("own", None),
        P("own", None),
        P(),
    )
    return jax.shard_map(
        per_device,
        mesh=mesh,
        in_specs=placed,
        out_specs=(P(None, "own"), P("own", None), P("own", None), P("own", None)),
        check_vma=False,
    )
```

time: 225 us -> 68.9 us (0.31)
  waiting for transfers between devices: 153 us -> 0 us
  Pallas kernels: 0 us -> 56.5 us
  starting transfers between devices: 27.5 us -> 0 us
  blocking collectives: 14 us -> 0 us
  between operations: 14.2 us -> 0.66 us
  other arithmetic: 8.92 us -> 0 us
  local copies, waits for them, and re-layouts: 3.86 us -> 11.3 us
  matrix products: 2.67 us -> 0 us
    all_to_all x2 -> x0, waiting for transfers between devices: 90.7 us -> none  [the longest x1 53.1 us: per_device(): lax.all_to_all(filled.reshape(slot_count, owner_count, piece_len), 'own',...]
    psum x1 -> x0, waiting for transfers between devices: 62 us -> none  [per_device(): summed, factor_sum = lax.psum((difference, factor), 'rep')]
    pallas_call x0 -> x1, Pallas kernels: none -> 56.5 us  [per_device(): pl.pallas_call(kernel, out_shape=(jax.ShapeDtypeStruct(anchor_dense.shape...]
    all_to_all x2 -> x0, starting transfers between devices: 27.5 us -> none  [the longest x1 18.9 us: per_device(): lax.all_to_all(filled.reshape(slot_count, owner_count, piece_len), 'own',...]
    psum x1 -> x0, blocking collectives: 14 us -> none  [per_device(): summed, factor_sum = lax.psum((difference, factor), 'rep')]
    unnamed x17 -> x20, local copies, waits for them, and re-layouts: 0.77 us -> 11.3 us
    sub x2 -> x0, other arithmetic: 2.99 us -> none  [the longest x1 2.11 us: per_device(): difference = anchor_dense - inner_dense[0]]
    dot_general x2 -> x0, matrix products: 2.67 us -> none  [the longest x1 1.77 us: per_device(): jnp.dot(emb_update, basis.T, precision=lax.Precision.HIGHEST, preferred_e...]
  transfers between devices with their start and end apart: 3 -> 0, of which waited for: 3 -> 0; matrix products, arithmetic and copies ran while one was open for 2% -> 0% of each run, Pallas kernels for 0% -> 0%
where the time goes in v1:
time: 68.9 us; the launch traced here: 68.5 us
  Pallas kernels  56.5 us (82%)
  local copies, waits for them, and re-layouts  11.3 us (16%)
    pallas_call x1, Pallas kernels, per_device(): pl.pallas_call(kernel, out_shape=(jax.ShapeDtypeStruct(anchor_dense.shape...  56.5 us
    unnamed x20, local copies, waits for them, and re-layouts  11.3 us

profile of v1, /device:TPU:1, one launch (start us, length us, event | category | flops | bytes accessed | tf_op | source)
XLA Modules:
  0.0 68.5 jit_solution(15163941141361375335)
XLA Ops:
  0.6 0.0 copy-start.7
  0.6 0.7 copy-done.7
  1.3 0.0 copy-start
  1.3 1.2 %copy-done = f32[4,65536]{1,0:T(4,128)S(1)} copy-done((f32[4,65536]{1,0:T(4,128)S(1)}, f32[4,65536]{1,0:T(4,128)}, u32[]{:S(2)}) %copy-start) | copy-done | bytes 1048600
  2.5 0.0 copy-start.1
  2.5 1.1 %copy-done.1 = f32[1,200,1024]{2,1,0:T(8,128)S(1)} copy-done((f32[1,200,1024]{2,1,0:T(8,128)S(1)}, f32[1,200,1024]{2,1,0:T(8,128)}, u32[]{:S(2)}) %copy-start.1) | copy-done | bytes 819224
  3.7 0.0 copy-start.2
  3.7 1.1 %copy-done.2 = f32[200,1024]{1,0:T(8,128)S(1)} copy-done((f32[200,1024]{1,0:T(8,128)S(1)}, f32[200,1024]{1,0:T(8,128)}, u32[]{:S(2)}) %copy-start.2) | copy-done | bytes 819224
  4.8 0.0 copy-start.3
  4.8 1.0 %copy-done.3 = f32[1,256,512]{2,1,0:T(8,128)S(1)} copy-done((f32[1,256,512]{2,1,0:T(8,128)S(1)}, f32[1,256,512]{2,1,0:T(8,128)}, u32[]{:S(2)}) %copy-start.3) | copy-done | bytes 524312
  5.9 0.0 copy-start.4
  5.9 1.0 %copy-done.4 = f32[256,512]{1,0:T(8,128)S(1)} copy-done((f32[256,512]{1,0:T(8,128)S(1)}, f32[256,512]{1,0:T(8,128)}, u32[]{:S(2)}) %copy-start.4) | copy-done | bytes 524312
  6.9 0.0 copy-start.5
  6.9 0.9 %copy-done.5 = f32[1024,64]{0,1:T(8,128)S(1)} copy-done((f32[1024,64]{0,1:T(8,128)S(1)}, f32[1024,64]{0,1:T(8,128)}, u32[]{:S(2)}) %copy-start.5) | copy-done | bytes 262168
  7.9 0.0 copy-start.6
  7.9 0.8 %copy-done.6 = f32[200,64]{0,1:T(8,128)S(1)} copy-done((f32[200,64]{0,1:T(8,128)S(1)}, f32[200,64]{0,1:T(8,128)}, u32[]{:S(2)}) %copy-start.6) | copy-done | bytes 51224
  8.7 56.5 %shard_map.111 = (f32[256,512]{1,0:T(8,128)S(1)}, f32[4,16,2,4,4,128]{5,4,3,2,1,0:T(4,128)S(1)}, f32[200,1024]{1,0:T(8,128)S(1)}, f32[64,200]{1,0:T(8,128)S(1)}) custom-call(s32[1,256]{1,0:T(1,128)S(1)} %bitcast.23, f32[256,512]{1,0:T(8,128)S(1)} %bitcast.19, f32[256,512]{1,0:T(8,128)S(1)} %copy-done.4, f32[4,16,2,4,4,128]{5,4,3,2,1,0:T(4,128)S(1)} %bitcast.16, ...), custom_call_target="tpu_custom_call" | custom-call | tf_op jit(solution)/shard_map/pallas_call | solution.py:299
  65.2 0.8 %copy.18 = f32[256,512]{1,0:T(8,128)} copy(f32[256,512]{1,0:T(8,128)S(1)} %get-tuple-element.16) | data formatting | bytes 1048576
  66.0 1.0 %copy.19 = f32[4,65536]{1,0:T(4,128)} copy(f32[4,65536]{1,0:T(4,128)S(1)} %bitcast.17) | data formatting | bytes 2097152
  67.0 0.9 %copy.20 = f32[200,1024]{1,0:T(8,128)} copy(f32[200,1024]{1,0:T(8,128)S(1)} %get-tuple-element.18) | data formatting | bytes 1638400
  67.9 0.6 copy.21
Async XLA Ops:
  0.6 0.7 copy-start.7
  1.3 1.2 %copy-start = (f32[4,65536]{1,0:T(4,128)S(1)}, f32[4,65536]{1,0:T(4,128)}, u32[]{:S(2)}) copy-start(f32[4,65536]{1,0:T(4,128)} %param.11) | copy-start | bytes 3145732
  2.5 1.1 %copy-start.1 = (f32[1,200,1024]{2,1,0:T(8,128)S(1)}, f32[1,200,1024]{2,1,0:T(8,128)}, u32[]{:S(2)}) copy-start(f32[1,200,1024]{2,1,0:T(8,128)} %param.12) | copy-start | bytes 2457604
  3.7 1.1 %copy-start.2 = (f32[200,1024]{1,0:T(8,128)S(1)}, f32[200,1024]{1,0:T(8,128)}, u32[]{:S(2)}) copy-start(f32[200,1024]{1,0:T(8,128)} %aemb_hbm.1) | copy-start | bytes 2457604
  4.8 1.0 %copy-start.3 = (f32[1,256,512]{2,1,0:T(8,128)S(1)}, f32[1,256,512]{2,1,0:T(8,128)}, u32[]{:S(2)}) copy-start(f32[1,256,512]{2,1,0:T(8,128)} %param.9) | copy-start | bytes 1572868
  5.9 1.0 %copy-start.4 = (f32[256,512]{1,0:T(8,128)S(1)}, f32[256,512]{1,0:T(8,128)}, u32[]{:S(2)}) copy-start(f32[256,512]{1,0:T(8,128)} %anchor_hbm.1) | copy-start | bytes 1572868
  6.9 0.9 %copy-start.5 = (f32[1024,64]{0,1:T(8,128)S(1)}, f32[1024,64]{0,1:T(8,128)}, u32[]{:S(2)}) copy-start(f32[1024,64]{0,1:T(8,128)} %param.15) | copy-start | bytes 786436
  7.9 0.8 %copy-start.6 = (f32[200,64]{0,1:T(8,128)S(1)}, f32[200,64]{0,1:T(8,128)}, u32[]{:S(2)}) copy-start(f32[200,64]{0,1:T(8,128)} %param.14) | copy-start | bytes 153604

commit v2 on v1

--- a/solution.py
+++ b/solution.py
@@ -12,9 +12,10 @@
 LANES = 128
 F32 = jnp.float32
 BF16 = jnp.bfloat16
-SEND_ORDER = (8, 7, 9, 6, 10, 5, 11, 4, 12, 3, 13, 2, 14, 1, 15)
-RANGES = ((6, 11), (3, 6), (11, 14), (14, 16), (0, 3))
-GROUPS_Z = ((0,), (1, 2), (3, 4))
+DISTANCE = (0, 1, 15, 2, 14, 3, 13, 4, 12, 5, 11, 6, 10, 7, 9, 8)
+M_GROUPS = ((13, 16), (9, 13), (0, 9))
+G_GROUPS = ((0, 5), (5, 9), (9, 13), (13, 16))
+G_PLANE = ((0, 9), (9, 16))
 
 
 def split3(v):
@@ -32,12 +33,17 @@
     return total + jnp.dot(onehot, high, preferred_element_type=F32)
 
 
+def slot_of_distance(e):
+    e = ((e + 8) & 15) - 8
+    return jnp.minimum(jnp.where(e > 0, 2 * e - 1, -2 * e), 15)
+
+
 def kernel(
     owners_hbm, inner_hbm, anchor_hbm, mom_hbm, iemb_hbm, aemb_hbm, memb_hbm, basis_hbm,
     nd_out, nm_out, ne_out, nme_out,
     owners, inq, anq, mom_v, ie, ae, memb, basis,
     rly, yin, gq, pack1, pick1, m1, m2, g0, g1, g2, fac,
-    loc, rs_recv, mz_recv, mp_recv, gz_recv, gp_recv, gy_recv, gf_recv, nd_recv, f_recv, snd,
+    loc, rs_recv, mz_recv, mp_recv, gp_recv, gz_recv, gy_recv, gf_recv, nd_recv, f_recv, snd,
 ):
     own = lax.axis_index("own")
     rep = lax.axis_index("rep")
@@ -51,8 +57,8 @@
     up = lax.rem(rep + 1, NR)
     down = lax.rem(rep + NR - 1, NR)
     across = lax.rem(rep + 2, NR)
-    z_at = [lax.rem(z + d, NZ) for d in range(NZ)]
-    z_peers = {d: {"rep": rep, "own": position(x, z_at[d], c)} for d in SEND_ORDER}
+    z_at = [lax.rem(z + d, NZ) for d in DISTANCE]
+    z_peers = [{"rep": rep, "own": position(x, at, c)} for at in z_at]
     plane = []
     for dx in range(NX):
         for dc in range(NC):
@@ -79,18 +85,20 @@
     def columns(r):
         return pl.ds(pl.multiple_of(r * LANES, LANES), LANES)
 
+    def run(ends):
+        return pl.ds(ends[0], ends[1] - ends[0])
+
     half = (pl.ds(0, 128), pl.ds(128, 128))
 
     barrier = pltpu.get_barrier_semaphore()
-    everyone = [z_peers[d] for d in SEND_ORDER] + [p[2] for p in plane]
-    everyone += [to_up, to_down, to_across]
+    everyone = z_peers[1:] + [p[2] for p in plane] + [to_up, to_down, to_across]
     for peer in everyone:
         pl.semaphore_signal(barrier, inc=1, device_id=peer, device_id_type=MESH)
 
     local(owners_hbm, owners, loc.at[0])
     local(inner_hbm.at[:, columns(rep)], inq, loc.at[1])
     local(anchor_hbm.at[:, columns(rep)], anq, loc.at[2])
-    local(mom_hbm.at[:, z, :, rep], m1.at[0], mz_recv.at[4])
+    local(mom_hbm.at[:, z, :, rep], m1.at[0], mz_recv.at[2])
     local(iemb_hbm, ie, loc.at[4])
     local(aemb_hbm, ae, loc.at[5])
     local(basis_hbm, basis, loc.at[6])
@@ -104,11 +112,9 @@
     send(inner_hbm.at[:, columns(up)], yin.at[0], snd.at[1], rs_recv.at[2], to_up)
     send(inner_hbm.at[:, columns(down)], yin.at[1], snd.at[1], rs_recv.at[3], to_down)
 
-    def range_of(d):
-        return next(i for i, (a, b) in enumerate(RANGES) if a <= d < b)
-
-    for d in SEND_ORDER:
-        send(mom_hbm.at[:, z_at[d], :, rep], m1.at[d], snd.at[2], mz_recv.at[range_of(d)], z_peers[d])
+    for group, (low, high) in enumerate(M_GROUPS):
+        for k in reversed(range(max(low, 1), high)):
+            send(mom_hbm.at[:, z_at[k], :, rep], m1.at[k], snd.at[2], mz_recv.at[group], z_peers[k])
 
     arrived(owners, loc.at[0])
     names = owners[...]
@@ -124,12 +130,12 @@
         return p >> 5, (p >> 1) & 15, p & 1
 
     ox, oz, oc = parts(names)
-    pack_row = ((((oz - z) & 15) * NX + ox) * NC + oc) * NS + slot_row
+    pack_row = ((ox * NC + oc) * NZ + slot_of_distance(oz - z)) * NS + slot_row
     pack1[...] = jnp.where(
         lax.broadcasted_iota(jnp.int32, (512, 256), 0) == pack_row, 1.0, 0.0
     ).astype(BF16)
     ox, oz, oc = parts(by_row[:, 0:1])
-    pick_column = ((ox * NZ + ((z - oz) & 15)) * NC + oc) * NS + slot_column
+    pick_column = ((ox * NC + oc) * NZ + slot_of_distance(z - oz)) * NS + slot_column
     pick1[...] = jnp.where(
         lax.broadcasted_iota(jnp.int32, (256, 512), 1) == pick_column, 1.0, 0.0
     ).astype(BF16)
@@ -158,36 +164,34 @@
     grad = (anchor - inq[...]) + (anchor - yin[0])
     grad = (grad + (anchor - yin[1]) + (anchor - yin[2])) * 0.25
     gq[...] = grad
-    g0[...] = select_rows(pack1[...], grad).reshape(NZ, NX, NC, NS, LANES)
-    for d in SEND_ORDER:
-        send(g0.at[d], g1.at[d], snd.at[4], gz_recv.at[range_of(d)], z_peers[d])
-    local(g0.at[0], g1.at[0], gz_recv.at[4])
+    g0[...] = select_rows(pack1[...], grad).reshape(NX, NC, NZ, NS, LANES)
+    for i, ends in enumerate(G_PLANE):
+        for px, pc, peer in plane:
+            send(g0.at[px, pc, run(ends)], g1.at[x, c, run(ends)], snd.at[4], gp_recv.at[i], peer)
+        local(g0.at[x, c, run(ends)], g1.at[x, c, run(ends)], gp_recv.at[i])
     for i, peer in enumerate((to_up, to_down, to_across)):
         send(fac.at[rep], fac.at[rep], snd.at[5], f_recv.at[i], peer)
 
-    def spread(src, dst, i, send_sem, recv_sem):
-        run = pl.ds(RANGES[i][0], RANGES[i][1] - RANGES[i][0])
+    def m_group(group):
+        ends = M_GROUPS[group]
+        arrived(m1.at[run(ends)], mz_recv.at[group])
         for px, pc, peer in plane:
-            send(src.at[run, px, pc], dst.at[x, run, c], send_sem, recv_sem, peer)
-        local(src.at[run, x, c], dst.at[x, run, c], recv_sem)
-
-    def run_of(i):
-        return pl.ds(RANGES[i][0], RANGES[i][1] - RANGES[i][0])
-
-    def m_group(group):
-        for i in GROUPS_Z[group]:
-            arrived(m1.at[run_of(i)], mz_recv.at[i])
-            spread(m1, m2, i, snd.at[6], mp_recv.at[i])
-
-    def g_group(group):
-        for i in GROUPS_Z[group]:
-            arrived(g1.at[run_of(i)], gz_recv.at[i])
-            spread(g1, g2.at[rep], i, snd.at[7], gp_recv.at[i])
-
-    for group in range(3):
-        m_group(group)
-    for i in range(len(RANGES)):
-        arrived(m2.at[:, run_of(i)], mp_recv.at[i])
+            send(m1.at[run(ends), px, pc], m2.at[x, c, run(ends)], snd.at[6], mp_recv.at[group], peer)
+        local(m1.at[run(ends), x, c], m2.at[x, c, run(ends)], mp_recv.at[group])
+
+    m_group(0)
+    m_group(1)
+    group_of = [next(i for i, (a, b) in enumerate(G_GROUPS) if a <= k < b) for k in range(NZ)]
+    for i, ends in enumerate(G_PLANE):
+        arrived(g1.at[:, :, run(ends)], gp_recv.at[i])
+        for k in range(max(ends[0], 1), ends[1]):
+            send(g1.at[:, :, k], g2.at[rep, k], snd.at[7], gz_recv.at[group_of[k]], z_peers[k])
+        if i == 0:
+            local(g1.at[:, :, 0], g2.at[rep, 0], gz_recv.at[0])
+    m_group(2)
+
+    for group, ends in enumerate(M_GROUPS):
+        arrived(m2.at[:, :, run(ends)], mp_recv.at[group])
     momentum = select_rows(pick1[...], m2[...].reshape(512, LANES))
     grad = gq[...]
     nd_out[:, columns(rep)] = anq[...] - RATE * (grad + DECAY * (DECAY * momentum + grad))
@@ -199,6 +203,23 @@
     send(nd_part(rep, 1), nd_part(rep, 1), snd.at[8], nd_recv.at[3], to_down)
     send(nd_part(rep, 1), nd_part(rep, 1), snd.at[8], nd_recv.at[1], to_up)
     send(nd_part(rep, 0), nd_part(rep, 0), snd.at[8], nd_recv.at[2], to_down)
+
+    def g_part(r, group, h):
+        return g2.at[r, run(G_GROUPS[group]), pl.ds(2 * h, 2)]
+
+    def g_share(group):
+        arrived(g2.at[rep, run(G_GROUPS[group])], gz_recv.at[group])
+        for h, sem, peer in ((0, 0, to_up), (1, 3, to_down), (1, 1, to_up), (0, 2, to_down)):
+            part = g_part(rep, group, h)
+            send(part, part, snd.at[10], gy_recv.at[group, sem], peer)
+
+    def g_relay(group):
+        arrived(g_part(down, group, 0), gy_recv.at[group, 0])
+        send(g_part(down, group, 0), g_part(down, group, 0), snd.at[11], gf_recv.at[group, 0], to_up)
+        arrived(g_part(up, group, 1), gy_recv.at[group, 3])
+        send(g_part(up, group, 1), g_part(up, group, 1), snd.at[11], gf_recv.at[group, 1], to_down)
+
+    g_share(0)
 
     arrived(memb, loc.at[7])
     arrived(fac.at[down], f_recv.at[0])
@@ -213,77 +234,63 @@
         precision=lax.Precision.HIGHEST, preferred_element_type=F32,
     )
 
-    g_group(0)
     arrived(nd_part(down, 0), nd_recv.at[0])
     send(nd_part(down, 0), nd_part(down, 0), snd.at[9], nd_recv.at[4], to_up)
     arrived(nd_part(up, 1), nd_recv.at[3])
     send(nd_part(up, 1), nd_part(up, 1), snd.at[9], nd_recv.at[5], to_down)
-
-    def g_part(r, i, h):
-        return g2.at[r, pl.ds(2 * h, 2), run_of(i)]
-
-    def g_share(group):
-        for i in GROUPS_Z[group]:
-            arrived(g2.at[rep, :, run_of(i)], gp_recv.at[i])
-            send(g_part(rep, i, 0), g_part(rep, i, 0), snd.at[10], gy_recv.at[i, 0], to_up)
-            send(g_part(rep, i, 1), g_part(rep, i, 1), snd.at[10], gy_recv.at[i, 3], to_down)
-            send(g_part(rep, i, 1), g_part(rep, i, 1), snd.at[10], gy_recv.at[i, 1], to_up)
-            send(g_part(rep, i, 0), g_part(rep, i, 0), snd.at[10], gy_recv.at[i, 2], to_down)
-
-    def g_relay(group):
-        for i in GROUPS_Z[group]:
-            arrived(g_part(down, i, 0), gy_recv.at[i, 0])
-            send(g_part(down, i, 0), g_part(down, i, 0), snd.at[11], gf_recv.at[i, 0], to_up)
-            arrived(g_part(up, i, 1), gy_recv.at[i, 3])
-            send(g_part(up, i, 1), g_part(up, i, 1), snd.at[11], gf_recv.at[i, 1], to_down)
-
-    g_group(1)
-    g_share(0)
-    g_group(2)
-    g_share(1)
     g_relay(0)
-    g_share(2)
-    g_relay(1)
-    g_relay(2)
+    for group in range(1, len(G_GROUPS)):
+        g_share(group)
+        if group > 1:
+            g_relay(group - 1)
+    g_relay(len(G_GROUPS) - 1)
 
     arrived(nd_part(down, 1), nd_recv.at[1])
     arrived(nd_part(up, 0), nd_recv.at[2])
     arrived(nd_part(across, 0), nd_recv.at[4])
     arrived(nd_part(across, 1), nd_recv.at[5])
     arrived(mom_v, loc.at[3])
-    for i in range(len(RANGES)):
-        arrived(g_part(down, i, 1), gy_recv.at[i, 1])
-        arrived(g_part(up, i, 0), gy_recv.at[i, 2])
-        arrived(g_part(across, i, 0), gf_recv.at[i, 0])
-        arrived(g_part(across, i, 1), gf_recv.at[i, 1])
-
     live = lax.broadcasted_iota(jnp.int32, (NS, LANES), 0) < owned
 
-    def finish(d, carry):
-        at = lax.rem(z + NZ - d, NZ)
+    def finish(k, carry):
+        steps = lax.div(k + 1, 2)
+        at = lax.rem(z + NZ + (1 - 2 * lax.rem(k, 2)) * steps, NZ)
         for px in range(NX):
             for pc in range(NC):
                 for r in range(NR):
-                    value = DECAY * mom_v[px, at, pc, r] + g2[r, px, d, pc]
+                    value = DECAY * mom_v[px, at, pc, r] + g2[r, k, px, pc]
                     nm_out[px, at, pc, r] = jnp.where(live, value, 0.0)
         return carry
 
-    lax.fori_loop(0, NZ, finish, 0)
+    for group, ends in enumerate(G_GROUPS):
+        arrived(g_part(down, group, 1), gy_recv.at[group, 1])
+        arrived(g_part(up, group, 0), gy_recv.at[group, 2])
+        arrived(g_part(across, group, 0), gf_recv.at[group, 0])
+        arrived(g_part(across, group, 1), gf_recv.at[group, 1])
+        lax.fori_loop(ends[0], ends[1], finish, 0)
 
     arrived(rly, snd.at[0])
     arrived(yin.at[pl.ds(0, 2)], snd.at[1])
     arrived(m1.at[pl.ds(1, 15)], snd.at[2])
     arrived(rly, snd.at[3])
-    arrived(g1.at[pl.ds(1, 15)], snd.at[4])
+    arrived(m1.at[pl.ds(0, 14)], snd.at[4])
     arrived(fac.at[pl.ds(0, 3)], snd.at[5])
-    arrived(m2.at[:, :, 0], snd.at[6])
-    arrived(m2.at[pl.ds(0, 3), :, 0], snd.at[6])
-    arrived(m2.at[:, :, 0], snd.at[7])
-    arrived(m2.at[pl.ds(0, 3), :, 0], snd.at[7])
+    arrived(m1.at[pl.ds(0, 14)], snd.at[6])
+    arrived(m1.at[pl.ds(1, 15)], snd.at[7])
     arrived(yin.at[pl.ds(0, 2)], snd.at[8])
     arrived(rly, snd.at[9])
     arrived(g2.at[pl.ds(0, 2)], snd.at[10])
     arrived(g2.at[0], snd.at[11])
+
+
+def store_out(*refs):
+    count = len(refs) // 2
+    sem = refs[-1]
+    copies = [pltpu.make_async_copy(refs[i], refs[count + i], sem.at[i]) for i in range(count)]
+    for copy in copies:
+        copy.start()
+    for copy in copies:
+        copy.wait()
 
 
 def per_device(
@@ -295,8 +302,7 @@
     vmem = pltpu.VMEM
     vocab, width = anchor_emb.shape
     rank = basis.shape[1]
-    ranges = len(RANGES)
-    new_dense, new_mom, new_emb, new_memb = pl.pallas_call(
+    results = pl.pallas_call(
         kernel,
         out_shape=(
             jax.ShapeDtypeStruct(anchor_dense.shape, F32),
@@ -321,19 +327,19 @@
             vmem((512, 256), BF16),
             vmem((256, 512), BF16),
             vmem((NZ, NX, NC, NS, LANES), F32),
-            vmem((NX, NZ, NC, NS, LANES), F32),
-            vmem((NZ, NX, NC, NS, LANES), F32),
-            vmem((NZ, NX, NC, NS, LANES), F32),
-            vmem((NR, NX, NZ, NC, NS, LANES), F32),
+            vmem((NX, NC, NZ, NS, LANES), F32),
+            vmem((NX, NC, NZ, NS, LANES), F32),
+            vmem((NX, NC, NZ, NS, LANES), F32),
+            vmem((NR, NZ, NX, NC, NS, LANES), F32),
             vmem((NR, rank, vocab), F32),
             dma((8,)),
             dma((6,)),
-            dma((ranges,)),
-            dma((ranges,)),
-            dma((ranges,)),
-            dma((ranges,)),
-            dma((ranges, 4)),
-            dma((ranges, 2)),
+            dma((len(M_GROUPS),)),
+            dma((len(M_GROUPS),)),
+            dma((len(G_PLANE),)),
+            dma((len(G_GROUPS),)),
+            dma((len(G_GROUPS), 4)),
+            dma((len(G_GROUPS), 2)),
             dma((6,)),
             dma((3,)),
             dma((12,)),
@@ -341,10 +347,21 @@
         compiler_params=pltpu.CompilerParams(
             collective_id=0, has_side_effects=True, vmem_limit_bytes=32 * 1024 * 1024
         ),
-    )(
-        owners.reshape(1, 256), inner_dense[0], anchor_dense, mom, inner_emb[0], anchor_emb,
-        momentum_emb.T, basis.T,
-    )
+    )(*[
+        pltpu.with_memory_space_constraint(v, pltpu.HBM)
+        for v in (
+            owners.reshape(1, 256), inner_dense[0], anchor_dense, mom, inner_emb[0], anchor_emb,
+            momentum_emb.T, basis.T,
+        )
+    ])
+    new_dense, new_mom, new_emb, new_memb = pl.pallas_call(
+        store_out,
+        out_shape=[jax.ShapeDtypeStruct(v.shape, v.dtype) for v in results],
+        in_specs=[pl.BlockSpec(memory_space=pltpu.VMEM)] * 4,
+        out_specs=[pl.BlockSpec(memory_space=pltpu.HBM)] * 4,
+        scratch_shapes=[dma((4,))],
+        compiler_params=pltpu.CompilerParams(vmem_limit_bytes=4 * 1024 * 1024),
+    )(*results)
     new_mom = new_mom.reshape(512, NS, LANES).transpose(1, 0, 2).reshape(momentum_dense.shape)
     return new_dense, new_mom, new_emb, new_memb.T
 

time: 68.9 us -> 55.4 us (0.80)
  the two profiles are of different devices: /device:TPU:1 before, /device:TPU:8 now
where the time goes in v2:
time: 55.4 us; the launch traced here: 55.3 us
  Pallas kernels  54.6 us (99%)
  between operations  0.64 us (1%)
    pallas_call x1, Pallas kernels, per_device(): pl.pallas_call(kernel, out_shape=(jax.ShapeDtypeStruct(anchor_dense.shape...  53.2 us
    pallas_call x1, Pallas kernels, per_device(): pl.pallas_call(store_out, out_shape=[jax.ShapeDtypeStruct(v.shape, v.dtyp...  1.45 us

profile of v2, /device:TPU:8, one launch (start us, length us, event | category | flops | bytes accessed | tf_op | source)
XLA Modules:
  0.0 55.3 jit_solution(12601554617388340344)
XLA Ops:
  0.6 53.2 %shard_map.111 = (f32[256,512]{1,0:T(8,128)S(1)}, f32[4,16,2,4,4,128]{5,4,3,2,1,0:T(4,128)S(1)}, f32[200,1024]{1,0:T(8,128)S(1)}, f32[64,200]{1,0:T(8,128)S(1)}) custom-call(s32[1,256]{1,0:T(1,128)} %bitcast.21, f32[256,512]{1,0:T(8,128)} %bitcast.18, f32[256,512]{1,0:T(8,128)} %anchor_hbm.1, f32[4,16,2,4,4,128]{5,4,3,2,1,0:T(4,128)} %bitcast.16, ...), custom_call_target="tpu_custom_call" | custom-call | tf_op jit(solution)/shard_map/pallas_call | solution.py:305
  53.8 1.5 %shard_map.112 = (f32[256,512]{1,0:T(8,128)}, f32[4,16,2,4,4,128]{5,4,3,2,1,0:T(4,128)}, f32[200,1024]{1,0:T(8,128)}, f32[64,200]{1,0:T(8,128)}) custom-call(f32[256,512]{1,0:T(8,128)S(1)} %get-tuple-element.12.refs_0_, f32[4,16,2,4,4,128]{5,4,3,2,1,0:T(4,128)S(1)} %get-tuple-element.13.refs_1_, f32[200,1024]{1,0:T(8,128)S(1)} %get-tuple-element.14.refs_2_, ...), custom_call_target="tpu_custom_call" | custom-call | tf_op jit(solution)/shard_map/pallas_call | solution.py:357

commit v3 on v2

--- a/solution.py
+++ b/solution.py
@@ -14,8 +14,9 @@
 BF16 = jnp.bfloat16
 DISTANCE = (0, 1, 15, 2, 14, 3, 13, 4, 12, 5, 11, 6, 10, 7, 9, 8)
 M_GROUPS = ((13, 16), (9, 13), (0, 9))
-G_GROUPS = ((0, 5), (5, 9), (9, 13), (13, 16))
-G_PLANE = ((0, 9), (9, 16))
+G_GROUPS = ((0, 5), (5, 9), (9, 13), (13, 15), (15, 16))
+G_PLANE = ((0, 5), (5, 16))
+DIRECT = 3
 
 
 def split3(v):
@@ -107,8 +108,7 @@
 
     pl.semaphore_wait(barrier, len(everyone))
 
-    send(inner_hbm.at[half[0], columns(across)], rly.at[0], snd.at[0], rs_recv.at[0], to_up)
-    send(inner_hbm.at[half[1], columns(across)], rly.at[1], snd.at[0], rs_recv.at[1], to_down)
+    send(inner_hbm.at[:, columns(across)], yin.at[2], snd.at[1], rs_recv.at[4], to_across)
     send(inner_hbm.at[:, columns(up)], yin.at[0], snd.at[1], rs_recv.at[2], to_up)
     send(inner_hbm.at[:, columns(down)], yin.at[1], snd.at[1], rs_recv.at[3], to_down)
 
@@ -141,11 +141,6 @@
     ).astype(BF16)
     owned = jnp.sum(jnp.where(names == own, 1, 0), axis=1, keepdims=True)
 
-    arrived(rly.at[0], rs_recv.at[0])
-    send(rly.at[0], yin.at[2, half[0]], snd.at[3], rs_recv.at[4], to_up)
-    arrived(rly.at[1], rs_recv.at[1])
-    send(rly.at[1], yin.at[2, half[1]], snd.at[3], rs_recv.at[5], to_down)
-
     arrived(ie, loc.at[4])
     arrived(ae, loc.at[5])
     arrived(basis, loc.at[6])
@@ -158,8 +153,7 @@
     arrived(anq, loc.at[2])
     arrived(yin.at[0], rs_recv.at[2])
     arrived(yin.at[1], rs_recv.at[3])
-    arrived(yin.at[2, half[0]], rs_recv.at[4])
-    arrived(yin.at[2, half[1]], rs_recv.at[5])
+    arrived(yin.at[2], rs_recv.at[4])
     anchor = anq[...]
     grad = (anchor - inq[...]) + (anchor - yin[0])
     grad = (grad + (anchor - yin[1]) + (anchor - yin[2])) * 0.25
@@ -209,11 +203,18 @@
 
     def g_share(group):
         arrived(g2.at[rep, run(G_GROUPS[group])], gz_recv.at[group])
+        if group >= DIRECT:
+            whole = g2.at[rep, run(G_GROUPS[group])]
+            for sem, peer in ((2, to_across), (0, to_up), (1, to_down)):
+                send(whole, whole, snd.at[12], gy_recv.at[group, sem], peer)
+            return
         for h, sem, peer in ((0, 0, to_up), (1, 3, to_down), (1, 1, to_up), (0, 2, to_down)):
             part = g_part(rep, group, h)
             send(part, part, snd.at[10], gy_recv.at[group, sem], peer)
 
     def g_relay(group):
+        if group >= DIRECT:
+            return
         arrived(g_part(down, group, 0), gy_recv.at[group, 0])
         send(g_part(down, group, 0), g_part(down, group, 0), snd.at[11], gf_recv.at[group, 0], to_up)
         arrived(g_part(up, group, 1), gy_recv.at[group, 3])
@@ -263,24 +264,28 @@
         return carry
 
     for group, ends in enumerate(G_GROUPS):
-        arrived(g_part(down, group, 1), gy_recv.at[group, 1])
-        arrived(g_part(up, group, 0), gy_recv.at[group, 2])
-        arrived(g_part(across, group, 0), gf_recv.at[group, 0])
-        arrived(g_part(across, group, 1), gf_recv.at[group, 1])
+        if group >= DIRECT:
+            for sem, r in enumerate((down, up, across)):
+                arrived(g2.at[r, run(ends)], gy_recv.at[group, sem])
+        else:
+            arrived(g_part(down, group, 1), gy_recv.at[group, 1])
+            arrived(g_part(up, group, 0), gy_recv.at[group, 2])
+            arrived(g_part(across, group, 0), gf_recv.at[group, 0])
+            arrived(g_part(across, group, 1), gf_recv.at[group, 1])
         lax.fori_loop(ends[0], ends[1], finish, 0)
 
-    arrived(rly, snd.at[0])
-    arrived(yin.at[pl.ds(0, 2)], snd.at[1])
+    arrived(yin, snd.at[1])
     arrived(m1.at[pl.ds(1, 15)], snd.at[2])
-    arrived(rly, snd.at[3])
     arrived(m1.at[pl.ds(0, 14)], snd.at[4])
     arrived(fac.at[pl.ds(0, 3)], snd.at[5])
     arrived(m1.at[pl.ds(0, 14)], snd.at[6])
     arrived(m1.at[pl.ds(1, 15)], snd.at[7])
     arrived(yin.at[pl.ds(0, 2)], snd.at[8])
     arrived(rly, snd.at[9])
-    arrived(g2.at[pl.ds(0, 2)], snd.at[10])
-    arrived(g2.at[0], snd.at[11])
+    early = pl.ds(0, G_GROUPS[DIRECT][0])
+    arrived(g2.at[pl.ds(0, 2), early], snd.at[10])
+    arrived(g2.at[0, early], snd.at[11])
+    arrived(g2.at[pl.ds(0, 3), run((G_GROUPS[DIRECT][0], NZ))], snd.at[12])
 
 
 def store_out(*refs):
@@ -342,7 +347,7 @@
             dma((len(G_GROUPS), 2)),
             dma((6,)),
             dma((3,)),
-            dma((12,)),
+            dma((13,)),
         ],
         compiler_params=pltpu.CompilerParams(
             collective_id=0, has_side_effects=True, vmem_limit_bytes=32 * 1024 * 1024

time: 55.4 us -> 53.5 us (0.966)
  the two profiles are of different devices: /device:TPU:8 before, /device:TPU:1 now
where the time goes in v3:
time: 53.5 us; the launch traced here: 53.4 us
  Pallas kernels  52.8 us (99%)
  between operations  0.64 us (1%)
    pallas_call x1, Pallas kernels, per_device(): pl.pallas_call(kernel, out_shape=(jax.ShapeDtypeStruct(anchor_dense.shape...  51.3 us
    pallas_call x1, Pallas kernels, per_device(): pl.pallas_call(store_out, out_shape=[jax.ShapeDtypeStruct(v.shape, v.dtyp...  1.45 us

profile of v3, /device:TPU:1, one launch (start us, length us, event | category | flops | bytes accessed | tf_op | source)
XLA Modules:
  0.0 53.4 jit_solution(2327347183427339764)
XLA Ops:
  0.6 51.3 %shard_map.111 = (f32[256,512]{1,0:T(8,128)S(1)}, f32[4,16,2,4,4,128]{5,4,3,2,1,0:T(4,128)S(1)}, f32[200,1024]{1,0:T(8,128)S(1)}, f32[64,200]{1,0:T(8,128)S(1)}) custom-call(s32[1,256]{1,0:T(1,128)} %bitcast.21, f32[256,512]{1,0:T(8,128)} %bitcast.18, f32[256,512]{1,0:T(8,128)} %anchor_hbm.1, f32[4,16,2,4,4,128]{5,4,3,2,1,0:T(4,128)} %bitcast.16, ...), custom_call_target="tpu_custom_call" | custom-call | tf_op jit(solution)/shard_map/pallas_call | solution.py:310
  52.0 1.5 %shard_map.112 = (f32[256,512]{1,0:T(8,128)}, f32[4,16,2,4,4,128]{5,4,3,2,1,0:T(4,128)}, f32[200,1024]{1,0:T(8,128)}, f32[64,200]{1,0:T(8,128)}) custom-call(f32[256,512]{1,0:T(8,128)S(1)} %get-tuple-element.12.refs_0_, f32[4,16,2,4,4,128]{5,4,3,2,1,0:T(4,128)S(1)} %get-tuple-element.13.refs_1_, f32[200,1024]{1,0:T(8,128)S(1)} %get-tuple-element.14.refs_2_, ...), custom_call_target="tpu_custom_call" | custom-call | tf_op jit(solution)/shard_map/pallas_call | solution.py:362

commit v4 on v3

--- a/solution.py
+++ b/solution.py
@@ -175,6 +175,7 @@
 
     m_group(0)
     m_group(1)
+    m_group(2)
     group_of = [next(i for i, (a, b) in enumerate(G_GROUPS) if a <= k < b) for k in range(NZ)]
     for i, ends in enumerate(G_PLANE):
         arrived(g1.at[:, :, run(ends)], gp_recv.at[i])
@@ -182,7 +183,6 @@
             send(g1.at[:, :, k], g2.at[rep, k], snd.at[7], gz_recv.at[group_of[k]], z_peers[k])
         if i == 0:
             local(g1.at[:, :, 0], g2.at[rep, 0], gz_recv.at[0])
-    m_group(2)
 
     for group, ends in enumerate(M_GROUPS):
         arrived(m2.at[:, :, run(ends)], mp_recv.at[group])

time: 53.5 us -> 53.6 us (level)
  no operation moved by 1% of the time
where the time goes in v4:
time: 53.6 us; the launch traced here: 53.4 us
  Pallas kernels  52.8 us (99%)
  between operations  0.64 us (1%)
    pallas_call x1, Pallas kernels, per_device(): pl.pallas_call(kernel, out_shape=(jax.ShapeDtypeStruct(anchor_dense.shape...  51.3 us
    pallas_call x1, Pallas kernels, per_device(): pl.pallas_call(store_out, out_shape=[jax.ShapeDtypeStruct(v.shape, v.dtyp...  1.45 us

profile of v4, /device:TPU:1, one launch (start us, length us, event | category | flops | bytes accessed | tf_op | source)
XLA Modules:
  0.0 53.4 jit_solution(13905980880537346179)
XLA Ops:
  0.6 51.3 %shard_map.111 = (f32[256,512]{1,0:T(8,128)S(1)}, f32[4,16,2,4,4,128]{5,4,3,2,1,0:T(4,128)S(1)}, f32[200,1024]{1,0:T(8,128)S(1)}, f32[64,200]{1,0:T(8,128)S(1)}) custom-call(s32[1,256]{1,0:T(1,128)} %bitcast.21, f32[256,512]{1,0:T(8,128)} %bitcast.18, f32[256,512]{1,0:T(8,128)} %anchor_hbm.1, f32[4,16,2,4,4,128]{5,4,3,2,1,0:T(4,128)} %bitcast.16, ...), custom_call_target="tpu_custom_call" | custom-call | tf_op jit(solution)/shard_map/pallas_call | solution.py:310
  52.0 1.5 %shard_map.112 = (f32[256,512]{1,0:T(8,128)}, f32[4,16,2,4,4,128]{5,4,3,2,1,0:T(4,128)}, f32[200,1024]{1,0:T(8,128)}, f32[64,200]{1,0:T(8,128)}) custom-call(f32[256,512]{1,0:T(8,128)S(1)} %get-tuple-element.12.refs_0_, f32[4,16,2,4,4,128]{5,4,3,2,1,0:T(4,128)S(1)} %get-tuple-element.13.refs_1_, f32[200,1024]{1,0:T(8,128)S(1)} %get-tuple-element.14.refs_2_, ...), custom_call_target="tpu_custom_call" | custom-call | tf_op jit(solution)/shard_map/pallas_call | solution.py:362
